TPU v7x, 512 devices: a whole 4x4x16 slice. The times are simulated.
512 devices in a mesh: blk: 16 (over y_hi, x, core), wide: 32 (over y_lo, z).
Axes of the slice: x: 4, y: 4 (y_hi: 2, y_lo: 2; y = y_hi * 2 + y_lo), z: 16, core: 2. Of those that a mesh axis runs over, the one named last changes fastest.
Arguments:
- patch_keys: float32 [512, 196, 512], P(('blk', 'wide')), may hold values from -16 to 16
- patch_values: float32 [512, 196, 512], P(('blk', 'wide')), may hold values from -6 to 6
- caption_queries: float32 [512, 512], P(('blk', 'wide')), may hold values from -48 to 48
- positive: int32 [512, 512], P(('blk', 'wide')), may hold values 0 or 1
Outputs:
- grad_keys: float32 [512, 196, 512], P(('blk', 'wide'))
- grad_values: float32 [512, 196, 512], P(('blk', 'wide'))
- grad_queries: float32 [512, 512], P(('blk', 'wide'))
All inputs are finite; a program needn't handle non-finite values. No bound on the sum of `positive` on one device may be relied on, other than what follows from the above.
Results may differ from a plain program's by a relative error of at most 0.0005.
Values sent between devices are 32-bit elements; how exact they have to be, the bound alone decides.
No kernel may reach another device: no remote copies, remote signals or barrier semaphores. Data moves between devices by JAX's collectives and lax.ppermute only.
A program may use at most 64 MiB of HBM per device.

v0:
```python
import jax
import jax.numpy as jnp
from jax import lax
from jax.sharding import PartitionSpec as P

HEADS = 8
epsilon = 1e-06
similarity_multiplier = 10.0
similarity_shift_term = -2.0


def passed_along(value, axis, steps):
    count = lax.axis_size(axis)
    pairs = [(source, (source + steps) % count) for source in range(count)]
    return lax.ppermute(value, axis, pairs)


def pair_loss(keys, values, queries, labels):
    images, patches, width = keys.shape
    row_count = queries.shape[0]
    head_dim = width // HEADS
    query_heads = queries.reshape(row_count, HEADS, head_dim)
    key_heads = keys.reshape(images, patches, HEADS, head_dim)
    value_heads = values.reshape(images, patches, HEADS, head_dim)
    scores = jnp.einsum(
        "chd,iphd->ichp", query_heads, key_heads, precision=lax.Precision.HIGHEST
    ) * head_dim ** (-0.5)
    row_max = lax.stop_gradient(jnp.max(scores, axis=3, keepdims=True))
    exponent = jnp.exp(scores - row_max)
    weights = exponent / jnp.sum(exponent, axis=3, keepdims=True)
    pooled = jnp.einsum(
        "ichp,iphd->ichd", weights, value_heads, precision=lax.Precision.HIGHEST
    ).reshape(images, row_count, width)
    matching_similarity = jnp.mean(pooled * queries[None], axis=2)
    summary_reciprocal_length = lax.rsqrt(jnp.mean(pooled * pooled, axis=2) + epsilon)
    probe_reciprocal_length = lax.rsqrt(jnp.mean(queries * queries, axis=1) + epsilon)
    matching_scaled_scores = (
        similarity_multiplier
        * matching_similarity
        * summary_reciprocal_length
        * probe_reciprocal_length[None]
        + similarity_shift_term
    )
    label_signs = 2.0 * labels.astype(jnp.float32) - 1.0
    return jnp.sum(jnp.logaddexp(0.0, -label_signs * matching_scaled_scores))


def pair_grads(keys, values, queries, labels):

    def loss_of(keys_in, values_in, input_queries):
        return pair_loss(keys_in, values_in, input_queries, labels)

    total, pull_back = jax.vjp(loss_of, keys, values, queries)
    return pull_back(jnp.ones_like(total))


def per_device(patch_keys, patch_values, caption_queries, positive):
    caption_group = lax.all_gather(caption_queries, "wide", axis=0, tiled=True)
    group_rows = caption_group.shape[0]
    cycle_size = lax.axis_size("blk")
    cycle_home = lax.axis_index("blk")
    key_zero = jnp.zeros_like(patch_keys)
    value_zero = jnp.zeros_like(patch_values)

    def cycle_turn(turn, carried):
        key_grad, value_grad, evaluate_objective, forward_acc, backward, backward_acc = carried
        source = (cycle_home - turn) % cycle_size
        labels_fwd = lax.dynamic_slice_in_dim(positive, source * group_rows, group_rows, 1)
        visiting = evaluate_objective
        key_part, value_part, query_part = pair_grads(
            patch_keys, patch_values, visiting, labels_fwd
        )
        forward_acc = forward_acc + query_part
        backward_acc = backward_acc + query_part[group_rows:]
        evaluate_objective, forward_acc = passed_along((evaluate_objective, forward_acc), "blk", 1)
        return (
            key_grad + key_part,
            value_grad + value_part,
            evaluate_objective,
            forward_acc,
            backward,
            backward_acc,
        )

    backward_start = caption_group[group_rows:]
    initial = (
        key_zero,
        value_zero,
        caption_group,
        jnp.zeros_like(caption_group),
        backward_start,
        jnp.zeros_like(backward_start),
    )
    grad_keys, grad_values, forward_end, forward_acc, backward_end, backward_acc = lax.fori_loop(
        0, cycle_size, cycle_turn, initial
    )
    group_grad = jnp.concatenate([forward_acc, backward_acc], 0)
    grad_queries = lax.psum_scatter(group_grad, "wide", scatter_dimension=0, tiled=True)
    return (grad_keys, grad_values, grad_queries)


def solution(mesh):
    in_specs = (
        P(("blk", "wide"), None, None),
        P(("blk", "wide"), None, None),
        P(("blk", "wide"), None),
        P(("blk", "wide"), None),
    )
    out_specs = (
        P(("blk", "wide"), None, None),
        P(("blk", "wide"), None, None),
        P(("blk", "wide"), None),
    )
    return jax.shard_map(
        per_device, mesh=mesh, in_specs=in_specs, out_specs=out_specs, check_vma=False
    )
```

profile of v0, /device:TPU:2, one launch (start us, length us, event | category | flops | bytes accessed | tf_op | source)
XLA Modules:
  0.0 610.4 jit_solution(129645985034968549)
XLA Ops:
  9.2 69.2 %all-gather = f32[32,1,512]{2,1,0:T(1,128)S(1)} all-gather(f32[1,1,512]{2,1,0:T(1,128)S(1)} %bitcast.248), channel_id=1, replica_groups=mesh['blk'=16,'wide'=32] {'wide'}, dimensions={0}, use_global_device_ids=true | all-gather | bytes 67584 | tf_op jit(solution)/shard_map/all_gather | solution.py:58
  79.6 283.0 %while.23 = (s32[]{:T(128)}, f32[1,196,512]{1,2,0:T(8,128)S(1)}, f32[1,196,512]{1,2,0:T(8,128)S(1)}, f32[32,512]{1,0:T(8,128)}, f32[32,512]{1,0:T(8,128)}, /*ind...) while((s32[]{:T(128)}, f32[1,196,512]{1,2,0:T(8,128)S(1)}, ...), condition=%wide.region_7.8_spmd.clone, body=%wide.region_0.7_spmd.clone.sunk | while | flops 232979744 | bytes 9337618 | solution.py:94
  88.2 3.5 collective-permute-start.1
  96.3 1.9 collective-permute-start
  104.0 3.2 collective-permute-start.1
  119.5 4.8 collective-permute-start.1
  136.6 5.7 collective-permute-start.1
  147.0 1.9 collective-permute-start
  154.7 5.7 collective-permute-start.1
  165.0 1.9 collective-permute-start
  172.7 5.7 collective-permute-start.1
  190.8 5.7 collective-permute-start.1
  208.8 5.7 collective-permute-start.1
  219.2 1.9 collective-permute-start
  226.8 5.7 collective-permute-start.1
  244.9 5.7 collective-permute-start.1
  262.9 5.7 collective-permute-start.1
  281.0 5.7 collective-permute-start.1
  299.0 5.7 collective-permute-start.1
  309.4 1.9 collective-permute-start
  317.1 5.7 collective-permute-start.1
  335.1 5.7 collective-permute-start.1
  353.2 5.7 collective-permute-start.1
  366.0 235.7 %all-reduce.3.cloned.1.call-done = f32[32,512]{1,0:T(8,128)} async-done(((f32[32,512]{1,0:T(8,128)}), f32[32,512]{1,0:T(8,128)}) %all-reduce.3.cloned.1.call-update) | async-done | bytes 65552
  (411 shorter events, 193.1 us)
Async XLA Ops:
  7.2 594.5 %all-reduce.3.cloned.1.call-start = ((), (), s32[]{:S(2)}) async-start(), calls=%async_computation | async-start | bytes 131072
  80.5 14.9 %collective-permute-start = (f32[32,512]{1,0:T(8,128)S(1)}, f32[32,512]{1,0:T(8,128)}, u32[]{:S(2)}, u32[]{:S(2)}) collective-permute-start(f32[32,512]{1,0:T(8,128)S(1)} %copy.71), channel_id=1, source_target_pairs={{0,32},{32,64},{64,96},{96,128},{128,160},{160,192},{192,224},{224... | collective-permute-start | bytes 196616 | tf_op jit(solution)/shard_map/while/body/eval_jaxpr/ppermute | solution.py:15
  96.3 14.7 %collective-permute-start = (f32[32,512]{1,0:T(8,128)S(1)}, f32[32,512]{1,0:T(8,128)}, u32[]{:S(2)}, u32[]{:S(2)}) collective-permute-start(f32[32,512]{1,0:T(8,128)S(1)} %copy.71), channel_id=1, source_target_pairs={{0,32},{32,64},{64,96},{96,128},{128,160},{160,192},{192,224},{224... | collective-permute-start | bytes 196616 | tf_op jit(solution)/shard_map/while/body/eval_jaxpr/ppermute | solution.py:15
  111.8 16.3 %collective-permute-start = (f32[32,512]{1,0:T(8,128)S(1)}, f32[32,512]{1,0:T(8,128)}, u32[]{:S(2)}, u32[]{:S(2)}) collective-permute-start(f32[32,512]{1,0:T(8,128)S(1)} %copy.71), channel_id=1, source_target_pairs={{0,32},{32,64},{64,96},{96,128},{128,160},{160,192},{192,224},{224... | collective-permute-start | bytes 196616 | tf_op jit(solution)/shard_map/while/body/eval_jaxpr/ppermute | solution.py:15
  128.9 17.2 %collective-permute-start = (f32[32,512]{1,0:T(8,128)S(1)}, f32[32,512]{1,0:T(8,128)}, u32[]{:S(2)}, u32[]{:S(2)}) collective-permute-start(f32[32,512]{1,0:T(8,128)S(1)} %copy.71), channel_id=1, source_target_pairs={{0,32},{32,64},{64,96},{96,128},{128,160},{160,192},{192,224},{224... | collective-permute-start | bytes 196616 | tf_op jit(solution)/shard_map/while/body/eval_jaxpr/ppermute | solution.py:15
  147.0 17.2 %collective-permute-start = (f32[32,512]{1,0:T(8,128)S(1)}, f32[32,512]{1,0:T(8,128)}, u32[]{:S(2)}, u32[]{:S(2)}) collective-permute-start(f32[32,512]{1,0:T(8,128)S(1)} %copy.71), channel_id=1, source_target_pairs={{0,32},{32,64},{64,96},{96,128},{128,160},{160,192},{192,224},{224... | collective-permute-start | bytes 196616 | tf_op jit(solution)/shard_map/while/body/eval_jaxpr/ppermute | solution.py:15
  154.7 9.5 %collective-permute-start.1 = (f32[32,512]{1,0:T(8,128)}, f32[32,512]{1,0:T(8,128)}, u32[]{:S(2)}, u32[]{:S(2)}) collective-permute-start(f32[32,512]{1,0:T(8,128)} %fusion.71), channel_id=1, source_target_pairs={{0,32},{32,64},{64,96},{96,128},{128,160},{160,192},{192,224},{224... | collective-permute-start | bytes 196616 | tf_op jit(solution)/shard_map/while/body/eval_jaxpr/ppermute | solution.py:15
  165.0 17.2 %collective-permute-start = (f32[32,512]{1,0:T(8,128)S(1)}, f32[32,512]{1,0:T(8,128)}, u32[]{:S(2)}, u32[]{:S(2)}) collective-permute-start(f32[32,512]{1,0:T(8,128)S(1)} %copy.71), channel_id=1, source_target_pairs={{0,32},{32,64},{64,96},{96,128},{128,160},{160,192},{192,224},{224... | collective-permute-start | bytes 196616 | tf_op jit(solution)/shard_map/while/body/eval_jaxpr/ppermute | solution.py:15
  183.1 17.2 %collective-permute-start = (f32[32,512]{1,0:T(8,128)S(1)}, f32[32,512]{1,0:T(8,128)}, u32[]{:S(2)}, u32[]{:S(2)}) collective-permute-start(f32[32,512]{1,0:T(8,128)S(1)} %copy.71), channel_id=1, source_target_pairs={{0,32},{32,64},{64,96},{96,128},{128,160},{160,192},{192,224},{224... | collective-permute-start | bytes 196616 | tf_op jit(solution)/shard_map/while/body/eval_jaxpr/ppermute | solution.py:15
  190.8 9.5 %collective-permute-start.1 = (f32[32,512]{1,0:T(8,128)}, f32[32,512]{1,0:T(8,128)}, u32[]{:S(2)}, u32[]{:S(2)}) collective-permute-start(f32[32,512]{1,0:T(8,128)} %fusion.71), channel_id=1, source_target_pairs={{0,32},{32,64},{64,96},{96,128},{128,160},{160,192},{192,224},{224... | collective-permute-start | bytes 196616 | tf_op jit(solution)/shard_map/while/body/eval_jaxpr/ppermute | solution.py:15
  201.1 17.2 %collective-permute-start = (f32[32,512]{1,0:T(8,128)S(1)}, f32[32,512]{1,0:T(8,128)}, u32[]{:S(2)}, u32[]{:S(2)}) collective-permute-start(f32[32,512]{1,0:T(8,128)S(1)} %copy.71), channel_id=1, source_target_pairs={{0,32},{32,64},{64,96},{96,128},{128,160},{160,192},{192,224},{224... | collective-permute-start | bytes 196616 | tf_op jit(solution)/shard_map/while/body/eval_jaxpr/ppermute | solution.py:15
  219.2 17.2 %collective-permute-start = (f32[32,512]{1,0:T(8,128)S(1)}, f32[32,512]{1,0:T(8,128)}, u32[]{:S(2)}, u32[]{:S(2)}) collective-permute-start(f32[32,512]{1,0:T(8,128)S(1)} %copy.71), channel_id=1, source_target_pairs={{0,32},{32,64},{64,96},{96,128},{128,160},{160,192},{192,224},{224... | collective-permute-start | bytes 196616 | tf_op jit(solution)/shard_map/while/body/eval_jaxpr/ppermute | solution.py:15
  226.8 9.5 %collective-permute-start.1 = (f32[32,512]{1,0:T(8,128)}, f32[32,512]{1,0:T(8,128)}, u32[]{:S(2)}, u32[]{:S(2)}) collective-permute-start(f32[32,512]{1,0:T(8,128)} %fusion.71), channel_id=1, source_target_pairs={{0,32},{32,64},{64,96},{96,128},{128,160},{160,192},{192,224},{224... | collective-permute-start | bytes 196616 | tf_op jit(solution)/shard_map/while/body/eval_jaxpr/ppermute | solution.py:15
  237.2 17.2 %collective-permute-start = (f32[32,512]{1,0:T(8,128)S(1)}, f32[32,512]{1,0:T(8,128)}, u32[]{:S(2)}, u32[]{:S(2)}) collective-permute-start(f32[32,512]{1,0:T(8,128)S(1)} %copy.71), channel_id=1, source_target_pairs={{0,32},{32,64},{64,96},{96,128},{128,160},{160,192},{192,224},{224... | collective-permute-start | bytes 196616 | tf_op jit(solution)/shard_map/while/body/eval_jaxpr/ppermute | solution.py:15
  255.2 17.2 %collective-permute-start = (f32[32,512]{1,0:T(8,128)S(1)}, f32[32,512]{1,0:T(8,128)}, u32[]{:S(2)}, u32[]{:S(2)}) collective-permute-start(f32[32,512]{1,0:T(8,128)S(1)} %copy.71), channel_id=1, source_target_pairs={{0,32},{32,64},{64,96},{96,128},{128,160},{160,192},{192,224},{224... | collective-permute-start | bytes 196616 | tf_op jit(solution)/shard_map/while/body/eval_jaxpr/ppermute | solution.py:15
  262.9 9.5 %collective-permute-start.1 = (f32[32,512]{1,0:T(8,128)}, f32[32,512]{1,0:T(8,128)}, u32[]{:S(2)}, u32[]{:S(2)}) collective-permute-start(f32[32,512]{1,0:T(8,128)} %fusion.71), channel_id=1, source_target_pairs={{0,32},{32,64},{64,96},{96,128},{128,160},{160,192},{192,224},{224... | collective-permute-start | bytes 196616 | tf_op jit(solution)/shard_map/while/body/eval_jaxpr/ppermute | solution.py:15
  273.3 17.2 %collective-permute-start = (f32[32,512]{1,0:T(8,128)S(1)}, f32[32,512]{1,0:T(8,128)}, u32[]{:S(2)}, u32[]{:S(2)}) collective-permute-start(f32[32,512]{1,0:T(8,128)S(1)} %copy.71), channel_id=1, source_target_pairs={{0,32},{32,64},{64,96},{96,128},{128,160},{160,192},{192,224},{224... | collective-permute-start | bytes 196616 | tf_op jit(solution)/shard_map/while/body/eval_jaxpr/ppermute | solution.py:15
  281.0 9.5 %collective-permute-start.1 = (f32[32,512]{1,0:T(8,128)}, f32[32,512]{1,0:T(8,128)}, u32[]{:S(2)}, u32[]{:S(2)}) collective-permute-start(f32[32,512]{1,0:T(8,128)} %fusion.71), channel_id=1, source_target_pairs={{0,32},{32,64},{64,96},{96,128},{128,160},{160,192},{192,224},{224... | collective-permute-start | bytes 196616 | tf_op jit(solution)/shard_map/while/body/eval_jaxpr/ppermute | solution.py:15
  291.3 17.2 %collective-permute-start = (f32[32,512]{1,0:T(8,128)S(1)}, f32[32,512]{1,0:T(8,128)}, u32[]{:S(2)}, u32[]{:S(2)}) collective-permute-start(f32[32,512]{1,0:T(8,128)S(1)} %copy.71), channel_id=1, source_target_pairs={{0,32},{32,64},{64,96},{96,128},{128,160},{160,192},{192,224},{224... | collective-permute-start | bytes 196616 | tf_op jit(solution)/shard_map/while/body/eval_jaxpr/ppermute | solution.py:15
  309.4 17.2 %collective-permute-start = (f32[32,512]{1,0:T(8,128)S(1)}, f32[32,512]{1,0:T(8,128)}, u32[]{:S(2)}, u32[]{:S(2)}) collective-permute-start(f32[32,512]{1,0:T(8,128)S(1)} %copy.71), channel_id=1, source_target_pairs={{0,32},{32,64},{64,96},{96,128},{128,160},{160,192},{192,224},{224... | collective-permute-start | bytes 196616 | tf_op jit(solution)/shard_map/while/body/eval_jaxpr/ppermute | solution.py:15
  317.1 9.5 %collective-permute-start.1 = (f32[32,512]{1,0:T(8,128)}, f32[32,512]{1,0:T(8,128)}, u32[]{:S(2)}, u32[]{:S(2)}) collective-permute-start(f32[32,512]{1,0:T(8,128)} %fusion.71), channel_id=1, source_target_pairs={{0,32},{32,64},{64,96},{96,128},{128,160},{160,192},{192,224},{224... | collective-permute-start | bytes 196616 | tf_op jit(solution)/shard_map/while/body/eval_jaxpr/ppermute | solution.py:15
  327.4 17.2 %collective-permute-start = (f32[32,512]{1,0:T(8,128)S(1)}, f32[32,512]{1,0:T(8,128)}, u32[]{:S(2)}, u32[]{:S(2)}) collective-permute-start(f32[32,512]{1,0:T(8,128)S(1)} %copy.71), channel_id=1, source_target_pairs={{0,32},{32,64},{64,96},{96,128},{128,160},{160,192},{192,224},{224... | collective-permute-start | bytes 196616 | tf_op jit(solution)/shard_map/while/body/eval_jaxpr/ppermute | solution.py:15
  345.5 17.2 %collective-permute-start = (f32[32,512]{1,0:T(8,128)S(1)}, f32[32,512]{1,0:T(8,128)}, u32[]{:S(2)}, u32[]{:S(2)}) collective-permute-start(f32[32,512]{1,0:T(8,128)S(1)} %copy.71), channel_id=1, source_target_pairs={{0,32},{32,64},{64,96},{96,128},{128,160},{160,192},{192,224},{224... | collective-permute-start | bytes 196616 | tf_op jit(solution)/shard_map/while/body/eval_jaxpr/ppermute | solution.py:15
  353.2 9.5 %collective-permute-start.1 = (f32[32,512]{1,0:T(8,128)}, f32[32,512]{1,0:T(8,128)}, u32[]{:S(2)}, u32[]{:S(2)}) collective-permute-start(f32[32,512]{1,0:T(8,128)} %fusion.71), channel_id=1, source_target_pairs={{0,32},{32,64},{64,96},{96,128},{128,160},{160,192},{192,224},{224... | collective-permute-start | bytes 196616 | tf_op jit(solution)/shard_map/while/body/eval_jaxpr/ppermute | solution.py:15
  (11 other events, 81.6 us)
Sparse Core Ops, SparseCore 0:
  362.8 238.8 all-reduce.2
where the time goes:
time: 614 us; the launch traced here: 610 us
  waiting for transfers between devices  236 us (38%)
  starting transfers between devices  117 us (19%)
  matrix products  76 us (12%)
  blocking collectives  69.2 us (11%)
  other arithmetic  65.8 us (11%)
  local copies, waits for them, and re-layouts  30.2 us (5%)
  between operations  14.1 us (2%)
    unnamed x2, waiting for transfers between devices  236 us
    ppermute x32, starting transfers between devices, passed_along(): return lax.ppermute(value, axis, pairs)  117 us
    all_gather x1, blocking collectives, per_device(): caption_group = lax.all_gather(caption_queries, 'wide', axis=0, tiled=True)  69.2 us
    dot_general x48, matrix products, pair_loss(): jnp.einsum('ichp,iphd->ichd', weights, value_heads, precision=lax.Precisi...  44.3 us
    dot_general x48, matrix products, pair_loss(): jnp.einsum('chd,iphd->ichp', query_heads, key_heads, precision=lax.Precis...  31.7 us
    add x16, other arithmetic, cycle_turn(): forward_acc = forward_acc + query_part  24.8 us
    add x16, other arithmetic, cycle_turn(): value_grad + value_part  22.3 us
    while x16, local copies, waits for them, and re-layouts  13.5 us
  transfers between devices with their start and end apart: 33, of which 1 were waited for; matrix products, arithmetic and copies ran while one was open for 25% of the time, Pallas kernels for 0%

commit v1 on v0

--- a/solution.py
+++ b/solution.py
@@ -55,7 +55,9 @@
 
 
 def per_device(patch_keys, patch_values, caption_queries, positive):
-    caption_group = lax.all_gather(caption_queries, "wide", axis=0, tiled=True)
+    caption_group = jnp.concatenate(
+        lax.all_to_all(jnp.stack([caption_queries] * lax.axis_size("wide")), "wide", 0, 0), axis=0
+    )
     group_rows = caption_group.shape[0]
     cycle_size = lax.axis_size("blk")
     cycle_home = lax.axis_index("blk")

time: 614 us -> 575 us (0.936)
  blocking collectives: 69.2 us -> 0 us
  starting transfers between devices: 117 us -> 133 us
  waiting for transfers between devices: 236 us -> 248 us
    all_gather x1 -> x0, blocking collectives: 69.2 us -> none  [per_device(): caption_group = lax.all_gather(caption_queries, 'wide', axis=0, tiled=True)]
    all_to_all x0 -> x1, starting transfers between devices: none -> 16.5 us  [per_device(): lax.all_to_all(jnp.stack([caption_queries] * lax.axis_size('wide')), 'wid...]
    all_to_all x0 -> x1, waiting for transfers between devices: none -> 12.4 us  [per_device(): lax.all_to_all(jnp.stack([caption_queries] * lax.axis_size('wide')), 'wid...]
  transfers between devices with their start and end apart: 33 -> 34, of which waited for: 1 -> 2; matrix products, arithmetic and copies ran while one was open for 25% -> 27% of each run, Pallas kernels for 0% -> 0%
where the time goes in v1:
time: 575 us; the launch traced here: 571 us
  waiting for transfers between devices  248 us (43%)
  starting transfers between devices  133 us (23%)
  matrix products  76 us (13%)
  other arithmetic  65.8 us (11%)
  local copies, waits for them, and re-layouts  31.3 us (5%)
  between operations  14.1 us (2%)
    unnamed x2, waiting for transfers between devices  236 us
    ppermute x32, starting transfers between devices, passed_along(): return lax.ppermute(value, axis, pairs)  117 us
    dot_general x48, matrix products, pair_loss(): jnp.einsum('ichp,iphd->ichd', weights, value_heads, precision=lax.Precisi...  44.3 us
    dot_general x48, matrix products, pair_loss(): jnp.einsum('chd,iphd->ichp', query_heads, key_heads, precision=lax.Precis...  31.7 us
    add x16, other arithmetic, cycle_turn(): forward_acc = forward_acc + query_part  24.8 us
    add x16, other arithmetic, cycle_turn(): value_grad + value_part  22.3 us
    all_to_all x1, starting transfers between devices, per_device(): lax.all_to_all(jnp.stack([caption_queries] * lax.axis_size('wide')), 'wid...  16.5 us
    while x16, local copies, waits for them, and re-layouts  13.5 us
  transfers between devices with their start and end apart: 34, of which 2 were waited for; matrix products, arithmetic and copies ran while one was open for 27% of the time, Pallas kernels for 0%

profile of v1, /device:TPU:2, one launch (start us, length us, event | category | flops | bytes accessed | tf_op | source)
XLA Modules:
  0.0 571.4 jit_solution(13017560659721302532)
XLA Ops:
  8.5 16.5 %all-to-all-start = ((f32[32,1,512]{2,1,0:T(1,128)}), f32[32,1,512]{2,1,0:T(1,128)S(1)}, u32[]{:S(2)}, u32[]{:S(2)}) async-start(f32[32,1,512]{2,1,0:T(1,128)} %stack.2), calls=%async_computation | async-start | bytes 131072 | tf_op jit(solution)/shard_map/all_to_all | solution.py:59
  26.9 12.4 %all-to-all-done = f32[32,1,512]{2,1,0:T(1,128)S(1)} async-done(((f32[32,1,512]{2,1,0:T(1,128)}), f32[32,1,512]{2,1,0:T(1,128)S(1)}, u32[]{:S(2)}, u32[]{:S(2)}) %all-to-all-start) | async-done | bytes 65568 | tf_op jit(solution)/shard_map/all_to_all | solution.py:59
  40.5 283.0 %while.23 = (s32[]{:T(128)}, f32[1,196,512]{1,2,0:T(8,128)S(1)}, f32[1,196,512]{1,2,0:T(8,128)S(1)}, f32[32,512]{1,0:T(8,128)}, f32[32,512]{1,0:T(8,128)}, /*ind...) while((s32[]{:T(128)}, f32[1,196,512]{1,2,0:T(8,128)S(1)}, ...), condition=%wide.region_7.8_spmd.clone, body=%wide.region_0.7_spmd.clone.sunk | while | flops 232979744 | bytes 9337618 | solution.py:96
  49.0 3.5 collective-permute-start.1
  64.8 3.2 collective-permute-start.1
  80.3 4.8 collective-permute-start.1
  97.5 5.7 %collective-permute-start.1 = (f32[32,512]{1,0:T(8,128)}, f32[32,512]{1,0:T(8,128)}, u32[]{:S(2)}, u32[]{:S(2)}) collective-permute-start(f32[32,512]{1,0:T(8,128)} %fusion.71), channel_id=1, source_target_pairs={{0,32},{32,64},{64,96},{96,128},{128,160},{160,192},{192,224},{224... | collective-permute-start | bytes 196616 | tf_op jit(solution)/shard_map/while/body/eval_jaxpr/ppermute | solution.py:15
  107.8 1.9 collective-permute-start
  115.5 5.7 %collective-permute-start.1 = (f32[32,512]{1,0:T(8,128)}, f32[32,512]{1,0:T(8,128)}, u32[]{:S(2)}, u32[]{:S(2)}) collective-permute-start(f32[32,512]{1,0:T(8,128)} %fusion.71), channel_id=1, source_target_pairs={{0,32},{32,64},{64,96},{96,128},{128,160},{160,192},{192,224},{224... | collective-permute-start | bytes 196616 | tf_op jit(solution)/shard_map/while/body/eval_jaxpr/ppermute | solution.py:15
  133.6 5.7 %collective-permute-start.1 = (f32[32,512]{1,0:T(8,128)}, f32[32,512]{1,0:T(8,128)}, u32[]{:S(2)}, u32[]{:S(2)}) collective-permute-start(f32[32,512]{1,0:T(8,128)} %fusion.71), channel_id=1, source_target_pairs={{0,32},{32,64},{64,96},{96,128},{128,160},{160,192},{192,224},{224... | collective-permute-start | bytes 196616 | tf_op jit(solution)/shard_map/while/body/eval_jaxpr/ppermute | solution.py:15
  143.9 1.9 collective-permute-start
  151.6 5.7 %collective-permute-start.1 = (f32[32,512]{1,0:T(8,128)}, f32[32,512]{1,0:T(8,128)}, u32[]{:S(2)}, u32[]{:S(2)}) collective-permute-start(f32[32,512]{1,0:T(8,128)} %fusion.71), channel_id=1, source_target_pairs={{0,32},{32,64},{64,96},{96,128},{128,160},{160,192},{192,224},{224... | collective-permute-start | bytes 196616 | tf_op jit(solution)/shard_map/while/body/eval_jaxpr/ppermute | solution.py:15
  161.9 1.9 collective-permute-start
  169.6 5.7 %collective-permute-start.1 = (f32[32,512]{1,0:T(8,128)}, f32[32,512]{1,0:T(8,128)}, u32[]{:S(2)}, u32[]{:S(2)}) collective-permute-start(f32[32,512]{1,0:T(8,128)} %fusion.71), channel_id=1, source_target_pairs={{0,32},{32,64},{64,96},{96,128},{128,160},{160,192},{192,224},{224... | collective-permute-start | bytes 196616 | tf_op jit(solution)/shard_map/while/body/eval_jaxpr/ppermute | solution.py:15
  187.7 5.7 %collective-permute-start.1 = (f32[32,512]{1,0:T(8,128)}, f32[32,512]{1,0:T(8,128)}, u32[]{:S(2)}, u32[]{:S(2)}) collective-permute-start(f32[32,512]{1,0:T(8,128)} %fusion.71), channel_id=1, source_target_pairs={{0,32},{32,64},{64,96},{96,128},{128,160},{160,192},{192,224},{224... | collective-permute-start | bytes 196616 | tf_op jit(solution)/shard_map/while/body/eval_jaxpr/ppermute | solution.py:15
  205.7 5.7 %collective-permute-start.1 = (f32[32,512]{1,0:T(8,128)}, f32[32,512]{1,0:T(8,128)}, u32[]{:S(2)}, u32[]{:S(2)}) collective-permute-start(f32[32,512]{1,0:T(8,128)} %fusion.71), channel_id=1, source_target_pairs={{0,32},{32,64},{64,96},{96,128},{128,160},{160,192},{192,224},{224... | collective-permute-start | bytes 196616 | tf_op jit(solution)/shard_map/while/body/eval_jaxpr/ppermute | solution.py:15
  223.8 5.7 %collective-permute-start.1 = (f32[32,512]{1,0:T(8,128)}, f32[32,512]{1,0:T(8,128)}, u32[]{:S(2)}, u32[]{:S(2)}) collective-permute-start(f32[32,512]{1,0:T(8,128)} %fusion.71), channel_id=1, source_target_pairs={{0,32},{32,64},{64,96},{96,128},{128,160},{160,192},{192,224},{224... | collective-permute-start | bytes 196616 | tf_op jit(solution)/shard_map/while/body/eval_jaxpr/ppermute | solution.py:15
  241.8 5.7 %collective-permute-start.1 = (f32[32,512]{1,0:T(8,128)}, f32[32,512]{1,0:T(8,128)}, u32[]{:S(2)}, u32[]{:S(2)}) collective-permute-start(f32[32,512]{1,0:T(8,128)} %fusion.71), channel_id=1, source_target_pairs={{0,32},{32,64},{64,96},{96,128},{128,160},{160,192},{192,224},{224... | collective-permute-start | bytes 196616 | tf_op jit(solution)/shard_map/while/body/eval_jaxpr/ppermute | solution.py:15
  252.2 1.9 collective-permute-start
  259.9 5.7 %collective-permute-start.1 = (f32[32,512]{1,0:T(8,128)}, f32[32,512]{1,0:T(8,128)}, u32[]{:S(2)}, u32[]{:S(2)}) collective-permute-start(f32[32,512]{1,0:T(8,128)} %fusion.71), channel_id=1, source_target_pairs={{0,32},{32,64},{64,96},{96,128},{128,160},{160,192},{192,224},{224... | collective-permute-start | bytes 196616 | tf_op jit(solution)/shard_map/while/body/eval_jaxpr/ppermute | solution.py:15
  277.9 5.7 %collective-permute-start.1 = (f32[32,512]{1,0:T(8,128)}, f32[32,512]{1,0:T(8,128)}, u32[]{:S(2)}, u32[]{:S(2)}) collective-permute-start(f32[32,512]{1,0:T(8,128)} %fusion.71), channel_id=1, source_target_pairs={{0,32},{32,64},{64,96},{96,128},{128,160},{160,192},{192,224},{224... | collective-permute-start | bytes 196616 | tf_op jit(solution)/shard_map/while/body/eval_jaxpr/ppermute | solution.py:15
  296.0 5.7 %collective-permute-start.1 = (f32[32,512]{1,0:T(8,128)}, f32[32,512]{1,0:T(8,128)}, u32[]{:S(2)}, u32[]{:S(2)}) collective-permute-start(f32[32,512]{1,0:T(8,128)} %fusion.71), channel_id=1, source_target_pairs={{0,32},{32,64},{64,96},{96,128},{128,160},{160,192},{192,224},{224... | collective-permute-start | bytes 196616 | tf_op jit(solution)/shard_map/while/body/eval_jaxpr/ppermute | solution.py:15
  314.0 5.7 %collective-permute-start.1 = (f32[32,512]{1,0:T(8,128)}, f32[32,512]{1,0:T(8,128)}, u32[]{:S(2)}, u32[]{:S(2)}) collective-permute-start(f32[32,512]{1,0:T(8,128)} %fusion.71), channel_id=1, source_target_pairs={{0,32},{32,64},{64,96},{96,128},{128,160},{160,192},{192,224},{224... | collective-permute-start | bytes 196616 | tf_op jit(solution)/shard_map/while/body/eval_jaxpr/ppermute | solution.py:15
  326.8 235.9 %all-reduce.3.cloned.1.call-done = f32[32,512]{1,0:T(8,128)} async-done(((f32[32,512]{1,0:T(8,128)}), f32[32,512]{1,0:T(8,128)}) %all-reduce.3.cloned.1.call-update) | async-done | bytes 65552
  (411 shorter events, 196.2 us)
Async XLA Ops:
  8.5 30.7 %all-to-all-start = ((f32[32,1,512]{2,1,0:T(1,128)}), f32[32,1,512]{2,1,0:T(1,128)S(1)}, u32[]{:S(2)}, u32[]{:S(2)}) async-start(f32[32,1,512]{2,1,0:T(1,128)} %stack.2), calls=%async_computation | async-start | bytes 131072 | tf_op jit(solution)/shard_map/all_to_all | solution.py:59
  25.0 537.7 %all-reduce.3.cloned.1.call-start = ((), (), s32[]{:S(2)}) async-start(), calls=%async_computation.1 | async-start | bytes 131072
  41.3 14.9 %collective-permute-start = (f32[32,512]{1,0:T(8,128)S(1)}, f32[32,512]{1,0:T(8,128)}, u32[]{:S(2)}, u32[]{:S(2)}) collective-permute-start(f32[32,512]{1,0:T(8,128)S(1)} %copy.71), channel_id=1, source_target_pairs={{0,32},{32,64},{64,96},{96,128},{128,160},{160,192},{192,224},{224... | collective-permute-start | bytes 196616 | tf_op jit(solution)/shard_map/while/body/eval_jaxpr/ppermute | solution.py:15
  57.1 14.6 %collective-permute-start = (f32[32,512]{1,0:T(8,128)S(1)}, f32[32,512]{1,0:T(8,128)}, u32[]{:S(2)}, u32[]{:S(2)}) collective-permute-start(f32[32,512]{1,0:T(8,128)S(1)} %copy.71), channel_id=1, source_target_pairs={{0,32},{32,64},{64,96},{96,128},{128,160},{160,192},{192,224},{224... | collective-permute-start | bytes 196616 | tf_op jit(solution)/shard_map/while/body/eval_jaxpr/ppermute | solution.py:15
  72.6 16.3 %collective-permute-start = (f32[32,512]{1,0:T(8,128)S(1)}, f32[32,512]{1,0:T(8,128)}, u32[]{:S(2)}, u32[]{:S(2)}) collective-permute-start(f32[32,512]{1,0:T(8,128)S(1)} %copy.71), channel_id=1, source_target_pairs={{0,32},{32,64},{64,96},{96,128},{128,160},{160,192},{192,224},{224... | collective-permute-start | bytes 196616 | tf_op jit(solution)/shard_map/while/body/eval_jaxpr/ppermute | solution.py:15
  89.8 17.2 %collective-permute-start = (f32[32,512]{1,0:T(8,128)S(1)}, f32[32,512]{1,0:T(8,128)}, u32[]{:S(2)}, u32[]{:S(2)}) collective-permute-start(f32[32,512]{1,0:T(8,128)S(1)} %copy.71), channel_id=1, source_target_pairs={{0,32},{32,64},{64,96},{96,128},{128,160},{160,192},{192,224},{224... | collective-permute-start | bytes 196616 | tf_op jit(solution)/shard_map/while/body/eval_jaxpr/ppermute | solution.py:15
  107.8 17.2 %collective-permute-start = (f32[32,512]{1,0:T(8,128)S(1)}, f32[32,512]{1,0:T(8,128)}, u32[]{:S(2)}, u32[]{:S(2)}) collective-permute-start(f32[32,512]{1,0:T(8,128)S(1)} %copy.71), channel_id=1, source_target_pairs={{0,32},{32,64},{64,96},{96,128},{128,160},{160,192},{192,224},{224... | collective-permute-start | bytes 196616 | tf_op jit(solution)/shard_map/while/body/eval_jaxpr/ppermute | solution.py:15
  125.9 17.2 %collective-permute-start = (f32[32,512]{1,0:T(8,128)S(1)}, f32[32,512]{1,0:T(8,128)}, u32[]{:S(2)}, u32[]{:S(2)}) collective-permute-start(f32[32,512]{1,0:T(8,128)S(1)} %copy.71), channel_id=1, source_target_pairs={{0,32},{32,64},{64,96},{96,128},{128,160},{160,192},{192,224},{224... | collective-permute-start | bytes 196616 | tf_op jit(solution)/shard_map/while/body/eval_jaxpr/ppermute | solution.py:15
  133.6 9.5 %collective-permute-start.1 = (f32[32,512]{1,0:T(8,128)}, f32[32,512]{1,0:T(8,128)}, u32[]{:S(2)}, u32[]{:S(2)}) collective-permute-start(f32[32,512]{1,0:T(8,128)} %fusion.71), channel_id=1, source_target_pairs={{0,32},{32,64},{64,96},{96,128},{128,160},{160,192},{192,224},{224... | collective-permute-start | bytes 196616 | tf_op jit(solution)/shard_map/while/body/eval_jaxpr/ppermute | solution.py:15
  143.9 17.2 %collective-permute-start = (f32[32,512]{1,0:T(8,128)S(1)}, f32[32,512]{1,0:T(8,128)}, u32[]{:S(2)}, u32[]{:S(2)}) collective-permute-start(f32[32,512]{1,0:T(8,128)S(1)} %copy.71), channel_id=1, source_target_pairs={{0,32},{32,64},{64,96},{96,128},{128,160},{160,192},{192,224},{224... | collective-permute-start | bytes 196616 | tf_op jit(solution)/shard_map/while/body/eval_jaxpr/ppermute | solution.py:15
  161.9 17.2 %collective-permute-start = (f32[32,512]{1,0:T(8,128)S(1)}, f32[32,512]{1,0:T(8,128)}, u32[]{:S(2)}, u32[]{:S(2)}) collective-permute-start(f32[32,512]{1,0:T(8,128)S(1)} %copy.71), channel_id=1, source_target_pairs={{0,32},{32,64},{64,96},{96,128},{128,160},{160,192},{192,224},{224... | collective-permute-start | bytes 196616 | tf_op jit(solution)/shard_map/while/body/eval_jaxpr/ppermute | solution.py:15
  169.6 9.5 %collective-permute-start.1 = (f32[32,512]{1,0:T(8,128)}, f32[32,512]{1,0:T(8,128)}, u32[]{:S(2)}, u32[]{:S(2)}) collective-permute-start(f32[32,512]{1,0:T(8,128)} %fusion.71), channel_id=1, source_target_pairs={{0,32},{32,64},{64,96},{96,128},{128,160},{160,192},{192,224},{224... | collective-permute-start | bytes 196616 | tf_op jit(solution)/shard_map/while/body/eval_jaxpr/ppermute | solution.py:15
  180.0 17.2 %collective-permute-start = (f32[32,512]{1,0:T(8,128)S(1)}, f32[32,512]{1,0:T(8,128)}, u32[]{:S(2)}, u32[]{:S(2)}) collective-permute-start(f32[32,512]{1,0:T(8,128)S(1)} %copy.71), channel_id=1, source_target_pairs={{0,32},{32,64},{64,96},{96,128},{128,160},{160,192},{192,224},{224... | collective-permute-start | bytes 196616 | tf_op jit(solution)/shard_map/while/body/eval_jaxpr/ppermute | solution.py:15
  198.0 17.2 %collective-permute-start = (f32[32,512]{1,0:T(8,128)S(1)}, f32[32,512]{1,0:T(8,128)}, u32[]{:S(2)}, u32[]{:S(2)}) collective-permute-start(f32[32,512]{1,0:T(8,128)S(1)} %copy.71), channel_id=1, source_target_pairs={{0,32},{32,64},{64,96},{96,128},{128,160},{160,192},{192,224},{224... | collective-permute-start | bytes 196616 | tf_op jit(solution)/shard_map/while/body/eval_jaxpr/ppermute | solution.py:15
  205.7 9.5 %collective-permute-start.1 = (f32[32,512]{1,0:T(8,128)}, f32[32,512]{1,0:T(8,128)}, u32[]{:S(2)}, u32[]{:S(2)}) collective-permute-start(f32[32,512]{1,0:T(8,128)} %fusion.71), channel_id=1, source_target_pairs={{0,32},{32,64},{64,96},{96,128},{128,160},{160,192},{192,224},{224... | collective-permute-start | bytes 196616 | tf_op jit(solution)/shard_map/while/body/eval_jaxpr/ppermute | solution.py:15
  216.1 17.2 %collective-permute-start = (f32[32,512]{1,0:T(8,128)S(1)}, f32[32,512]{1,0:T(8,128)}, u32[]{:S(2)}, u32[]{:S(2)}) collective-permute-start(f32[32,512]{1,0:T(8,128)S(1)} %copy.71), channel_id=1, source_target_pairs={{0,32},{32,64},{64,96},{96,128},{128,160},{160,192},{192,224},{224... | collective-permute-start | bytes 196616 | tf_op jit(solution)/shard_map/while/body/eval_jaxpr/ppermute | solution.py:15
  223.8 9.5 %collective-permute-start.1 = (f32[32,512]{1,0:T(8,128)}, f32[32,512]{1,0:T(8,128)}, u32[]{:S(2)}, u32[]{:S(2)}) collective-permute-start(f32[32,512]{1,0:T(8,128)} %fusion.71), channel_id=1, source_target_pairs={{0,32},{32,64},{64,96},{96,128},{128,160},{160,192},{192,224},{224... | collective-permute-start | bytes 196616 | tf_op jit(solution)/shard_map/while/body/eval_jaxpr/ppermute | solution.py:15
  234.1 17.2 %collective-permute-start = (f32[32,512]{1,0:T(8,128)S(1)}, f32[32,512]{1,0:T(8,128)}, u32[]{:S(2)}, u32[]{:S(2)}) collective-permute-start(f32[32,512]{1,0:T(8,128)S(1)} %copy.71), channel_id=1, source_target_pairs={{0,32},{32,64},{64,96},{96,128},{128,160},{160,192},{192,224},{224... | collective-permute-start | bytes 196616 | tf_op jit(solution)/shard_map/while/body/eval_jaxpr/ppermute | solution.py:15
  252.2 17.2 %collective-permute-start = (f32[32,512]{1,0:T(8,128)S(1)}, f32[32,512]{1,0:T(8,128)}, u32[]{:S(2)}, u32[]{:S(2)}) collective-permute-start(f32[32,512]{1,0:T(8,128)S(1)} %copy.71), channel_id=1, source_target_pairs={{0,32},{32,64},{64,96},{96,128},{128,160},{160,192},{192,224},{224... | collective-permute-start | bytes 196616 | tf_op jit(solution)/shard_map/while/body/eval_jaxpr/ppermute | solution.py:15
  259.9 9.5 %collective-permute-start.1 = (f32[32,512]{1,0:T(8,128)}, f32[32,512]{1,0:T(8,128)}, u32[]{:S(2)}, u32[]{:S(2)}) collective-permute-start(f32[32,512]{1,0:T(8,128)} %fusion.71), channel_id=1, source_target_pairs={{0,32},{32,64},{64,96},{96,128},{128,160},{160,192},{192,224},{224... | collective-permute-start | bytes 196616 | tf_op jit(solution)/shard_map/while/body/eval_jaxpr/ppermute | solution.py:15
  270.2 17.2 %collective-permute-start = (f32[32,512]{1,0:T(8,128)S(1)}, f32[32,512]{1,0:T(8,128)}, u32[]{:S(2)}, u32[]{:S(2)}) collective-permute-start(f32[32,512]{1,0:T(8,128)S(1)} %copy.71), channel_id=1, source_target_pairs={{0,32},{32,64},{64,96},{96,128},{128,160},{160,192},{192,224},{224... | collective-permute-start | bytes 196616 | tf_op jit(solution)/shard_map/while/body/eval_jaxpr/ppermute | solution.py:15
  288.3 17.2 %collective-permute-start = (f32[32,512]{1,0:T(8,128)S(1)}, f32[32,512]{1,0:T(8,128)}, u32[]{:S(2)}, u32[]{:S(2)}) collective-permute-start(f32[32,512]{1,0:T(8,128)S(1)} %copy.71), channel_id=1, source_target_pairs={{0,32},{32,64},{64,96},{96,128},{128,160},{160,192},{192,224},{224... | collective-permute-start | bytes 196616 | tf_op jit(solution)/shard_map/while/body/eval_jaxpr/ppermute | solution.py:15
  296.0 9.5 %collective-permute-start.1 = (f32[32,512]{1,0:T(8,128)}, f32[32,512]{1,0:T(8,128)}, u32[]{:S(2)}, u32[]{:S(2)}) collective-permute-start(f32[32,512]{1,0:T(8,128)} %fusion.71), channel_id=1, source_target_pairs={{0,32},{32,64},{64,96},{96,128},{128,160},{160,192},{192,224},{224... | collective-permute-start | bytes 196616 | tf_op jit(solution)/shard_map/while/body/eval_jaxpr/ppermute | solution.py:15
  306.3 17.2 %collective-permute-start = (f32[32,512]{1,0:T(8,128)S(1)}, f32[32,512]{1,0:T(8,128)}, u32[]{:S(2)}, u32[]{:S(2)}) collective-permute-start(f32[32,512]{1,0:T(8,128)S(1)} %copy.71), channel_id=1, source_target_pairs={{0,32},{32,64},{64,96},{96,128},{128,160},{160,192},{192,224},{224... | collective-permute-start | bytes 196616 | tf_op jit(solution)/shard_map/while/body/eval_jaxpr/ppermute | solution.py:15
  (11 other events, 90.4 us)
Sparse Core Ops, SparseCore 0:
  323.6 238.9 all-reduce.2
